TPU v7x, 32 devices: a whole 2x2x4 slice. The times are simulated.
32 devices in a mesh: dp: 8 (over z, x), fsdp: 4 (over y, core).
Axes of the slice: x: 2, y: 2, z: 4, core: 2. Of those that a mesh axis runs over, the one named last changes fastest.
Arguments:
- tokens: bfloat16 [16384, 768], P(('dp', 'fsdp')), may hold values from -6 to 6
- cotangent: bfloat16 [16384, 768], P(('dp', 'fsdp')), may hold values from -6 to 6
- lengths: int32 [32], P(('dp', 'fsdp')), may hold values from 128 to 512
- rel_1d: int32 [32, 512, 512], P(('dp', 'fsdp')), may hold values from 0 to 31
- rel_x: int32 [32, 512, 512], P(('dp', 'fsdp')), may hold values from 0 to 63
- rel_y: int32 [32, 512, 512], P(('dp', 'fsdp')), may hold values from 0 to 63
- attn_weights: float32 [3072, 768], P(('dp', 'fsdp')), may hold values from -0.25 to 0.25
- attn_m1: float32 [3072, 768], P(('dp', 'fsdp')), may hold values from -0.00061035156 to 0.00061035156
- attn_m2: float32 [3072, 768], P(('dp', 'fsdp')), may hold values from 1.4106315e-10 to 5.642526e-10
- attn_ema: float32 [3072, 768], P(('dp', 'fsdp')), may hold values from -0.25 to 0.25
- ffn_weights: float32 [6144, 768], P(('dp', 'fsdp')), may hold values from -0.0625 to 0.0625
- ffn_m1: float32 [6144, 768], P(('dp', 'fsdp')), may hold values from -0.00061035156 to 0.00061035156
- ffn_m2: float32 [6144, 768], P(('dp', 'fsdp')), may hold values from 1.4106315e-10 to 5.642526e-10
- ffn_ema: float32 [6144, 768], P(('dp', 'fsdp')), may hold values from -0.0625 to 0.0625
- vectors: float32 [12, 768], replicated, may hold values from -0.8 to 1.5, as said below
- vec_m1: float32 [12, 768], replicated, may hold values from -0.0024414062 to 0.0024414062
- vec_m2: float32 [12, 768], replicated, may hold values from 2.2570104e-09 to 9.028041e-09
- vec_ema: float32 [12, 768], replicated, may hold values from -0.8 to 1.5, as said below
- table: float32 [160, 12], replicated, may hold values from -5 to 5
- tab_m1: float32 [160, 12], replicated, may hold values from -0.0007324219 to 0.0007324219
- tab_m2: float32 [160, 12], replicated, may hold values from 1.4106315e-10 to 5.642526e-10
- tab_ema: float32 [160, 12], replicated, may hold values from -5 to 5
Outputs:
- block_out: bfloat16 [16384, 768], P(('dp', 'fsdp'))
- grad_input: float32 [16384, 768], P(('dp', 'fsdp'))
- grad_norm: float32 [], replicated
- new_attn: float32 [3072, 768], P(('dp', 'fsdp'))
- new_attn_m1: float32 [3072, 768], P(('dp', 'fsdp'))
- new_attn_m2: float32 [3072, 768], P(('dp', 'fsdp'))
- new_attn_ema: float32 [3072, 768], P(('dp', 'fsdp'))
- new_ffn: float32 [6144, 768], P(('dp', 'fsdp'))
- new_ffn_m1: float32 [6144, 768], P(('dp', 'fsdp'))
- new_ffn_m2: float32 [6144, 768], P(('dp', 'fsdp'))
- new_ffn_ema: float32 [6144, 768], P(('dp', 'fsdp'))
- new_vectors: float32 [12, 768], replicated
- new_vec_m1: float32 [12, 768], replicated
- new_vec_m2: float32 [12, 768], replicated
- new_vec_ema: float32 [12, 768], replicated
- new_table: float32 [160, 12], replicated
- new_tab_m1: float32 [160, 12], replicated
- new_tab_m2: float32 [160, 12], replicated
- new_tab_ema: float32 [160, 12], replicated
- vec_grad: float32 [12, 768], replicated
Inputs may be any that keep to these rules, and one draw needn't show every extreme that they name: `vectors`: rows 0 and 2 lie in 0.5 to 1.5. `vec_ema`: rows 0 and 2 lie in 0.5 to 1.5.
All inputs are finite; a program needn't handle non-finite values.
Results may differ from a plain program's by a relative error of at most 0.017.
Values may be sent and summed in bfloat16 or wider, within the bound.
No kernel may reach another device: no remote copies, remote signals or barrier semaphores. Data moves between devices by JAX's collectives and lax.ppermute only.
A program may use at most 128 MiB of HBM per device.

v0:
```python
import math

import jax
import jax.numpy as jnp
from jax import lax
from jax.sharding import PartitionSpec as P

D = 768
H = 12
HD = 64
FF = 3072
B1 = 32
BX = 64
SEQ = 512
STEP = 10


NEG_FILL = -1e30
NORM_EPS = 1e-05


def norm_rows(values, gain_row, shift_row):
    center = values - jnp.mean(values, axis=-1, keepdims=True)
    spread = jnp.mean(center * center, axis=-1, keepdims=True)
    return center * lax.rsqrt(spread + NORM_EPS) * gain_row + shift_row


def exact_gelu(values):
    return jax.nn.gelu(values, approximate=False)


def adam_update(weight, moment_one, second, gradient, clip_scale, step_rate, decay_rate, average):
    clipped = gradient * clip_scale
    new_first = 0.9 * moment_one + 0.1 * clipped
    new_second = 0.999 * second + 0.001 * clipped * clipped
    first_hat = new_first / (1.0 - 0.9**STEP)
    second_hat = new_second / (1.0 - 0.999**STEP)
    new_weight = weight - step_rate * (
        first_hat / (jnp.sqrt(second_hat) + 1e-08) + decay_rate * weight
    )
    new_average = 0.8 * average + 0.2 * new_weight
    return (new_weight, new_first, new_second, new_average)


def bucket_onehot(one_rows, x_rows, y_rows):
    bucket_ids = jnp.arange(B1 + 2 * BX, dtype=jnp.int32)
    first_hot = (one_rows[..., None] == bucket_ids).astype(jnp.bfloat16)
    second_hot = (x_rows[..., None] + B1 == bucket_ids).astype(jnp.bfloat16)
    third_hot = (y_rows[..., None] + B1 + BX == bucket_ids).astype(jnp.bfloat16)
    return first_hot + second_hot + third_hot


def rel_bias(one_idx, x_idx, y_idx, bias_table):
    row_block = math.gcd(SEQ, 32)
    table_high = bias_table.astype(jnp.bfloat16)
    table_rest = (bias_table - table_high.astype(jnp.float32)).astype(jnp.bfloat16)

    def rel_one_block(block_start):
        first_rows = lax.dynamic_slice_in_dim(one_idx, block_start * row_block, row_block, 0)
        second_rows = lax.dynamic_slice_in_dim(x_idx, block_start * row_block, row_block, 0)
        third_rows = lax.dynamic_slice_in_dim(y_idx, block_start * row_block, row_block, 0)
        one_hot = bucket_onehot(first_rows, second_rows, third_rows)
        upper = jnp.einsum("ijb,bh->ihj", one_hot, table_high, preferred_element_type=jnp.float32)
        lower = jnp.einsum("ijb,bh->ihj", one_hot, table_rest, preferred_element_type=jnp.float32)
        return upper + lower

    blocks = lax.map(rel_one_block, jnp.arange(SEQ // row_block))
    return blocks.reshape(SEQ, H, SEQ)


def table_grad(one_idx, x_idx, y_idx, d_scores):
    row_block = math.gcd(SEQ, 32)

    def table_one_block(block_start):
        first_rows = lax.dynamic_slice_in_dim(one_idx, block_start * row_block, row_block, 0)
        second_rows = lax.dynamic_slice_in_dim(x_idx, block_start * row_block, row_block, 0)
        third_rows = lax.dynamic_slice_in_dim(y_idx, block_start * row_block, row_block, 0)
        one_hot = bucket_onehot(first_rows, second_rows, third_rows)
        d_block = lax.dynamic_slice_in_dim(d_scores, block_start * row_block, row_block, 0)
        return jnp.einsum("ijb,ihj->bh", one_hot, d_block, preferred_element_type=jnp.float32)

    return jnp.sum(lax.map(table_one_block, jnp.arange(SEQ // row_block)), axis=0)


def split_weights(attn_full, ffn_full):
    return (attn_full[: 3 * D].reshape(3, D, D), attn_full[3 * D :], ffn_full[:FF], ffn_full[FF:])


def shards(
    tokens,
    cotangent,
    lengths,
    rel_1d,
    rel_x,
    rel_y,
    attn_weights,
    attn_m1,
    attn_m2,
    attn_ema,
    ffn_weights,
    ffn_m1,
    ffn_m2,
    ffn_ema,
    vectors,
    vec_m1,
    vec_m2,
    vec_ema,
    table,
    tab_m1,
    tab_m2,
    tab_ema,
):
    page_count = tokens.shape[0] // SEQ
    scaling = HD ** (-0.5)
    contract_last = (((1,), (1,)), ((), ()))
    contract_first = (((0,), (0,)), ((), ()))
    attn_full, ffn_full = (
        lax.all_gather(attn_weights.astype(jnp.bfloat16), ("dp", "fsdp"), axis=0, tiled=True),
        lax.all_gather(ffn_weights.astype(jnp.bfloat16), ("dp", "fsdp"), axis=0, tiled=True),
    )
    w_three, w_out, w_first, w_second = split_weights(attn_full, ffn_full)
    gain_one, shift_one, gain_two, shift_two = (vectors[0], vectors[1], vectors[2], vectors[3])
    bias_q, bias_v, bias_o, bias_two = (vectors[4], vectors[5], vectors[6], vectors[7])
    bias_first = vectors[8:].reshape(FF)

    def to_pages(rows):
        return rows.reshape(page_count, SEQ, H, HD)

    x_float = tokens.astype(jnp.float32)
    projected = jnp.einsum("si,tio->sto", tokens, w_three, preferred_element_type=jnp.float32)
    queries = (projected[:, 0] + bias_q).astype(jnp.bfloat16)
    key_rows = projected[:, 1].astype(jnp.bfloat16)
    value_rows = (projected[:, 2] + bias_v).astype(jnp.bfloat16)

    def attend_page(operands):
        page_q, page_k, page_v, page_len, one_idx, x_idx, y_idx = operands
        bias_page = rel_bias(one_idx, x_idx, y_idx, table)
        scores = (
            jnp.einsum("ihd,jhd->ihj", page_q, page_k, preferred_element_type=jnp.float32) * scaling
            + bias_page
        )
        scores = jnp.where(jnp.arange(SEQ, dtype=jnp.int32) < page_len, scores, NEG_FILL)
        top_score = jnp.max(scores, axis=-1, keepdims=True)
        raised = jnp.exp(scores - top_score)
        row_total = jnp.sum(raised, axis=-1, keepdims=True)
        weights_soft = raised / row_total
        log_total = top_score + jnp.log(row_total)
        context = jnp.einsum(
            "ihj,jhd->ihd",
            weights_soft.astype(jnp.bfloat16),
            page_v,
            preferred_element_type=jnp.float32,
        )
        return (context.astype(jnp.bfloat16), log_total, bias_page)

    context_pages, log_totals, bias_pages = lax.map(
        attend_page,
        (
            to_pages(queries),
            to_pages(key_rows),
            to_pages(value_rows),
            lengths,
            rel_1d,
            rel_x,
            rel_y,
        ),
    )
    context_rows = context_pages.reshape(-1, D)
    attn_lin = jnp.dot(context_rows, w_out, preferred_element_type=jnp.float32) + bias_o
    resid_one = x_float + attn_lin
    hidden = norm_rows(resid_one, gain_one, shift_one)
    hidden_low = hidden.astype(jnp.bfloat16)
    pre_act = (
        lax.dot_general(hidden_low, w_first, contract_last, preferred_element_type=jnp.float32)
        + bias_first
    )
    act_low = exact_gelu(pre_act).astype(jnp.bfloat16)
    ffn_out = jnp.dot(act_low, w_second, preferred_element_type=jnp.float32) + bias_two
    resid_two = hidden + ffn_out
    block_out = norm_rows(resid_two, gain_two, shift_two).astype(jnp.bfloat16)
    attn_back, ffn_back = (
        lax.all_gather(attn_weights.astype(jnp.bfloat16), ("dp", "fsdp"), axis=0, tiled=True),
        lax.all_gather(ffn_weights.astype(jnp.bfloat16), ("dp", "fsdp"), axis=0, tiled=True),
    )
    w_three, w_out, w_first, w_second = split_weights(attn_back, ffn_back)
    d_out = cotangent.astype(jnp.float32)
    unused_two, norm_back_two = jax.vjp(norm_rows, resid_two, gain_two, shift_two)
    d_resid_two, d_gain_two, d_shift_two = norm_back_two(d_out)
    d_ffn = d_resid_two.astype(jnp.bfloat16)
    grad_second = lax.dot_general(
        act_low, d_ffn, contract_first, preferred_element_type=jnp.float32
    )
    grad_bias_two = jnp.sum(d_ffn.astype(jnp.float32), axis=0)
    d_act = lax.dot_general(d_ffn, w_second, contract_last, preferred_element_type=jnp.float32)
    unused_gelu, gelu_back = jax.vjp(exact_gelu, pre_act)
    d_pre_low = gelu_back(d_act)[0].astype(jnp.bfloat16)
    grad_first = lax.dot_general(
        d_pre_low, hidden_low, contract_first, preferred_element_type=jnp.float32
    )
    grad_bias_first = jnp.sum(d_pre_low.astype(jnp.float32), axis=0)
    grad_ffn = jnp.concatenate([grad_first, grad_second], axis=0)
    d_hidden = d_resid_two + jnp.dot(d_pre_low, w_first, preferred_element_type=jnp.float32)
    unused_one, norm_back_one = jax.vjp(norm_rows, resid_one, gain_one, shift_one)
    d_resid_one, d_gain_one, d_shift_one = norm_back_one(d_hidden)
    d_attn = d_resid_one.astype(jnp.bfloat16)
    grad_out_w = lax.dot_general(
        context_rows, d_attn, contract_first, preferred_element_type=jnp.float32
    )
    grad_bias_o = jnp.sum(d_attn.astype(jnp.float32), axis=0)
    d_context = lax.dot_general(
        d_attn, w_out, contract_last, preferred_element_type=jnp.float32
    ).astype(jnp.bfloat16)

    def attend_back(operands):
        page_q, page_k, page_v, page_len, log_total, bias_page, page_dctx, one_idx, x_idx, y_idx = (
            operands
        )
        scores = (
            jnp.einsum("ihd,jhd->ihj", page_q, page_k, preferred_element_type=jnp.float32) * scaling
            + bias_page
        )
        scores = jnp.where(jnp.arange(SEQ, dtype=jnp.int32) < page_len, scores, NEG_FILL)
        weights_soft = jnp.exp(scores - log_total)
        d_weights = jnp.einsum(
            "ihd,jhd->ihj", page_dctx, page_v, preferred_element_type=jnp.float32
        )
        d_values = jnp.einsum(
            "ihj,ihd->jhd",
            weights_soft.astype(jnp.bfloat16),
            page_dctx,
            preferred_element_type=jnp.float32,
        ).astype(jnp.bfloat16)
        inner = jnp.sum(weights_soft * d_weights, axis=-1, keepdims=True)
        d_scores = (weights_soft * (d_weights - inner)).astype(jnp.bfloat16)
        d_queries = (
            jnp.einsum("ihj,jhd->ihd", d_scores, page_k, preferred_element_type=jnp.float32)
            * scaling
        ).astype(jnp.bfloat16)
        d_keys = (
            jnp.einsum("ihj,ihd->jhd", d_scores, page_q, preferred_element_type=jnp.float32)
            * scaling
        ).astype(jnp.bfloat16)
        return (d_queries, d_keys, d_values, table_grad(one_idx, x_idx, y_idx, d_scores))

    dq_pages, dk_pages, dv_pages, table_pages = lax.map(
        attend_back,
        (
            to_pages(queries),
            to_pages(key_rows),
            to_pages(value_rows),
            lengths,
            log_totals,
            bias_pages,
            to_pages(d_context),
            rel_1d,
            rel_x,
            rel_y,
        ),
    )
    d_three = jnp.stack(
        [dq_pages.reshape(-1, D), dk_pages.reshape(-1, D), dv_pages.reshape(-1, D)], axis=1
    )
    grad_three = jnp.einsum("si,sto->tio", tokens, d_three, preferred_element_type=jnp.float32)
    grad_input = d_resid_one + jnp.einsum(
        "sto,tio->si", d_three, w_three, preferred_element_type=jnp.float32
    )
    grad_bias_q = jnp.sum(d_three[:, 0].astype(jnp.float32), axis=0)
    grad_bias_v = jnp.sum(d_three[:, 2].astype(jnp.float32), axis=0)
    grad_table = jnp.sum(table_pages, axis=0)
    grad_attn = jnp.concatenate([grad_three.reshape(3 * D, D), grad_out_w], axis=0)
    attn_shard, ffn_shard = (
        lax.psum_scatter(grad_attn, ("dp", "fsdp"), scatter_dimension=0, tiled=True),
        lax.psum_scatter(grad_ffn, ("dp", "fsdp"), scatter_dimension=0, tiled=True),
    )
    grad_vectors = jnp.concatenate(
        [
            jnp.stack(
                [
                    d_gain_one,
                    d_shift_one,
                    d_gain_two,
                    d_shift_two,
                    grad_bias_q,
                    grad_bias_v,
                    grad_bias_o,
                    grad_bias_two,
                ]
            ),
            grad_bias_first.reshape(FF // D, D),
        ],
        axis=0,
    )
    shard_squares = jnp.sum(attn_shard * attn_shard) + jnp.sum(ffn_shard * ffn_shard)
    vec_total, tab_total, square_total = lax.psum(
        (grad_vectors, grad_table, shard_squares), ("dp", "fsdp")
    )
    grad_norm = jnp.sqrt(
        square_total + jnp.sum(vec_total * vec_total) + jnp.sum(tab_total * tab_total)
    )
    clip_scale = 1.0 / jnp.maximum(grad_norm, 1.0)
    attn_new = adam_update(
        attn_weights, attn_m1, attn_m2, attn_shard, clip_scale, 0.06, 0.01, attn_ema
    )
    ffn_new = adam_update(ffn_weights, ffn_m1, ffn_m2, ffn_shard, clip_scale, 0.06, 0.01, ffn_ema)
    vec_new = adam_update(vectors, vec_m1, vec_m2, vec_total, clip_scale, 0.6, 0.0, vec_ema)
    tab_new = adam_update(table, tab_m1, tab_m2, tab_total, clip_scale, 0.6, 0.0, tab_ema)
    return (
        block_out,
        grad_input,
        grad_norm,
        attn_new[0],
        attn_new[1],
        attn_new[2],
        attn_new[3],
        ffn_new[0],
        ffn_new[1],
        ffn_new[2],
        ffn_new[3],
        vec_new[0],
        vec_new[1],
        vec_new[2],
        vec_new[3],
        tab_new[0],
        tab_new[1],
        tab_new[2],
        tab_new[3],
        vec_total * clip_scale,
    )


def solution(mesh):
    return jax.shard_map(
        shards,
        mesh=mesh,
        in_specs=(
            P(("dp", "fsdp"), None),
            P(("dp", "fsdp"), None),
            P(("dp", "fsdp")),
            P(("dp", "fsdp"), None, None),
            P(("dp", "fsdp"), None, None),
            P(("dp", "fsdp"), None, None),
            P(("dp", "fsdp"), None),
            P(("dp", "fsdp"), None),
            P(("dp", "fsdp"), None),
            P(("dp", "fsdp"), None),
            P(("dp", "fsdp"), None),
            P(("dp", "fsdp"), None),
            P(("dp", "fsdp"), None),
            P(("dp", "fsdp"), None),
            P(),
            P(),
            P(),
            P(),
            P(),
            P(),
            P(),
            P(),
        ),
        out_specs=(
            P(("dp", "fsdp"), None),
            P(("dp", "fsdp"), None),
            P(),
            P(("dp", "fsdp"), None),
            P(("dp", "fsdp"), None),
            P(("dp", "fsdp"), None),
            P(("dp", "fsdp"), None),
            P(("dp", "fsdp"), None),
            P(("dp", "fsdp"), None),
            P(("dp", "fsdp"), None),
            P(("dp", "fsdp"), None),
            P(),
            P(),
            P(),
            P(),
            P(),
            P(),
            P(),
            P(),
            P(),
        ),
        check_vma=False,
    )
```

profile of v0, /device:TPU:0, one launch (start us, length us, event | category | flops | bytes accessed | tf_op | source)
XLA Modules:
  0.0 736.5 jit_solution(10268867719099546566)
XLA Ops:
  12.4 160.9 %while.43 = (s32[]{:T(128)}, f32[16,32,12,512]{3,2,1,0:T(8,128)}, s32[16]{0:T(128)S(1)}, s32[512,512]{1,0:T(8,128)}, s32[512,512]{1,0:T(8,128)}, /*index=5*/s32[...) while((s32[]{:T(128)}, f32[16,32,12,512]{3,2,1,0:T(8,128)}, ...), condition=%wide.region_1.2_spmd, body=%wide.region_0.1_spmd.sunk | while | flops 188973056 | bytes 3415747 | solution.py:67
  18.4 4.1 fusion.142
  28.4 4.1 fusion.142
  38.5 4.1 fusion.142
  48.6 4.1 fusion.142
  58.6 4.1 fusion.142
  68.6 4.1 fusion.142
  78.7 4.1 fusion.142
  88.8 4.1 fusion.142
  98.8 4.2 fusion.142
  108.9 4.1 fusion.142
  119.0 4.1 fusion.142
  139.0 4.1 fusion.142
  149.2 4.1 fusion.142
  159.2 4.1 fusion.142
  169.2 4.1 fusion.142
  173.3 16.9 %copy.62 = f32[512,12,512]{0,2,1:T(8,128)} copy(f32[512,12,512]{2,1,0:T(8,128)} %bitcast.100) | data formatting | bytes 25165824 | tf_op jit(solution)/shard_map/while/body/eval_jaxpr/reshape | solution.py:68
  206.6 7.3 fusion.105
  225.3 20.1 %multiply_convert_fusion = (bf16[512,3072]{1,0:T(8,128)(2,1)S(1)}, f32[512,3072]{1,0:T(8,128)S(1)}, f32[512,3072]{1,0:T(8,128)}) fusion(f32[3072]{0:T(1024)S(1)} %add.335, bf16[6144,768]{1,0:T(8,128)(2,1)} %all-gather.5.cloned.1.call-done, f32[512,768]{1,0:T(8,128)} %copy-done.4, f32[768]{0:T(1024)S(1)} %get-tuple-element.315, ...), kind=kOutput, calls=%fused_computation.57 | convolution fusion | flops 2521694208 | bytes 22042624 | tf_op jit(solution)/shard_map/dot_general | solution.py:174
  251.0 6.9 convert_reduce_fusion
  267.4 7.7 %convert_reduce_fusion.4 = (f32[12,64]{1,0:T(8,128)S(1)}, bf16[12,64,512]{2,1,0:T(8,128)(2,1)}) fusion(bf16[512,12,64]{0,2,1:T(8,128)(2,1)S(1)} %bitcast.105, f32[512,12,512]{0,2,1:T(8,128)} %copy-done, f32[512,12]{0,1:T(8,128)S(1)} %log_add_fusion), kind=kOutput, calls=%fused_computation.94 | convolution fusion | flops 410123520 | bytes 14183424 | tf_op jit(solution)/shard_map/while/body/eval_jaxpr/ihj,ihd->jhd/dot_general | solution.py:227
  275.1 9.0 %fusion.40 = (f32[512,12]{0,1:T(8,128)S(1)}, f32[12,512,512]{2,1,0:T(8,128)}) fusion(f32[512,12,512]{0,2,1:T(8,128)} %copy-done, f32[512,12]{0,1:T(8,128)S(1)} %log_add_fusion, bf16[512,12,64]{0,2,1:T(8,128)(2,1)S(1)} %bitcast.106, f32[512,12,64]{0,2,1:T(8,128)S(1)} %bitcast.110, f32[12,64]{1,0:T(8,128)S(1)} %add.320), kind=kOutput, calls=%fused_computation.40 | convolution fusion | flops 412870656 | bytes 27577344 | tf_op jit(solution)/shard_map/while/body/eval_jaxpr/ihd,jhd->ihj/dot_general | solution.py:224
  284.1 6.8 fusion.42
  301.8 6.8 fusion.81
  308.6 7.3 pad_maximum_fusion.1
  317.1 4.7 fusion.109
  324.6 10.7 %pad_maximum_fusion = f32[6144,768]{1,0:T(8,128)} fusion(f32[3072,768]{1,0:T(8,128)S(1)} %fusion.109, f32[3072,768]{1,0:T(8,128)S(1)} %fusion.94), kind=kLoop, calls=%fused_computation.37 | loop fusion | flops 4718592 | bytes 37748736 | tf_op jit(solution)/shard_map/concatenate | solution.py:201
  335.4 14.7 %copy.72 = bf16[512,12,512]{2,1,0:T(8,128)(2,1)} copy(bf16[512,12,512]{0,2,1:T(8,128)(2,1)} %copy-done.1) | data formatting | bytes 12582912 | tf_op jit(solution)/shard_map/while/body/eval_jaxpr/while | solution.py:82
  350.3 112.5 %while.44 = (s32[]{:T(128)}, f32[16,160,12]{1,2,0:T(8,128)S(1)}, s32[16]{0:T(128)S(1)}, s32[512,512]{1,0:T(8,128)}, s32[512,512]{1,0:T(8,128)}, /*index=5*/s32[5...) while((s32[]{:T(128)}, f32[16,160,12]{1,2,0:T(8,128)S(1)}, ...), condition=%wide.region_30.31_spmd, body=%wide.region_29.30_spmd.sunk | while | flops 94404616 | bytes 1130687 | solution.py:82
  464.5 202.7 %reduce-scatter.5.cloned.1.call-done = f32[192,768]{1,0:T(8,128)} async-done(((f32[6144,768]{1,0:T(8,128)}), f32[192,768]{1,0:T(8,128)}) %reduce-scatter.5.cloned.1.call-update) | async-done | bytes 589840 | tf_op jit(solution)/shard_map/reduce_scatter | solution.py:273
  670.4 6.0 bitcast_add_fusion.1
  676.4 40.4 %all-reduce = (f32[]{:T(128)}, f32[12,768]{1,0:T(8,128)S(1)}, f32[160,12]{0,1:T(8,128)S(1)}) all-reduce(f32[]{:T(128)S(6)} %add.349, f32[12,768]{1,0:T(8,128)S(1)} %concatenate.11, f32[160,12]{0,1:T(8,128)S(1)} %reduce_sum.256), channel_id=1, replica_groups=mesh['dp'=8,'fsdp'=4] {'dp','fsdp'}, use_global_device_ids=true, to_apply=%region_17.18 | all-reduce | flops 11137 | bytes 89096 | tf_op jit(solution)/shard_map/psum | solution.py:294
  (284 shorter events, 266.0 us)
Async XLA Ops:
  7.2 184.0 %all-gather.3.cloned.1.call-start = ((), (), s32[]{:S(2)}) async-start(), calls=%async_computation.2 | async-start | bytes 4866048 | tf_op jit(solution)/shard_map/all_gather | solution.py:118
  8.9 216.3 %all-gather.5.cloned.1.call-start = ((), (), s32[]{:S(2)}) async-start(), calls=%async_computation.3 | async-start | bytes 9732096 | tf_op jit(solution)/shard_map/all_gather | solution.py:119
  10.8 452.1 %reduce-scatter.3.cloned.1.call-start = ((), (), s32[]{:S(2)}) async-start(), calls=%async_computation.4 | async-start | bytes 9732096 | tf_op jit(solution)/shard_map/reduce_scatter | solution.py:272
  173.3 16.9 %copy-start.22 = (f32[12,768]{1,0:T(8,128)S(1)}, f32[12,768]{1,0:T(8,128)}, u32[]{:S(2)}) copy-start(f32[12,768]{1,0:T(8,128)} %param.40) | copy-start | bytes 110596
  190.2 3.2 copy-start.30
  214.0 4.7 copy-start
  214.0 4.7 copy-start.2
  221.2 4.0 copy-start.20
  225.3 20.2 %copy-start.5 = (f32[512,768]{1,0:T(8,128)S(1)}, f32[512,768]{1,0:T(8,128)}, u32[]{:S(2)}) copy-start(f32[512,768]{1,0:T(8,128)} %copy-done.4) | copy-start | bytes 4718596
  225.3 20.2 %copy-start.29 = (bf16[6144,768]{1,0:T(8,128)(2,1)S(1)}, bf16[6144,768]{1,0:T(8,128)(2,1)}, u32[]{:S(2)}) copy-start(bf16[6144,768]{1,0:T(8,128)(2,1)} %all-gather.5.cloned.1.call-done) | copy-start | bytes 28311556
  245.5 3.1 copy-start.11
  251.0 6.9 copy-start.18
  257.9 3.0 copy-start.32
  261.6 5.8 copy-start.28
  267.4 7.7 %copy-start.3 = (f32[512,1,768]{0,2,1:T(8,128)S(1)}, f32[512,1,768]{0,2,1:T(8,128)}, u32[]{:S(2)}) copy-start(f32[512,1,768]{0,2,1:T(8,128)} %copy.58) | copy-start | bytes 4718596
  267.4 16.7 %slice-start = ((s8[12582912]{0:T(1024)(128)(4,1)}), s8[4194304]{0:T(1024)(128)(4,1)S(1)}, s32[]{:S(2)}) async-start(s8[12582912]{0:T(1024)(128)(4,1)} %bitcast.98), calls=%async_computation.6 | async-start | bytes 8388608
  267.4 16.7 %slice-start.1 = ((s8[12582912]{0:T(1024)(128)(4,1)}), s8[4194304]{0:T(1024)(128)(4,1)S(1)}, s32[]{:S(2)}) async-start(s8[12582912]{0:T(1024)(128)(4,1)} %bitcast.98), calls=%async_computation.7 | async-start | bytes 8388608
  275.1 9.0 %slice-start.2 = ((s8[12582912]{0:T(1024)(128)(4,1)}), s8[4194304]{0:T(1024)(128)(4,1)S(1)}, s32[]{:S(2)}) async-start(s8[12582912]{0:T(1024)(128)(4,1)} %bitcast.98), calls=%async_computation.8 | async-start | bytes 8388608
  291.0 4.1 copy-start.1
  316.0 5.8 copy-start.6
  316.0 351.2 %reduce-scatter.5.cloned.1.call-start = ((), (), s32[]{:S(2)}) async-start(), calls=%async_computation.5 | async-start | bytes 19464192 | tf_op jit(solution)/shard_map/reduce_scatter | solution.py:273
  317.1 4.7 copy-start.33
  350.3 320.0 %copy-start.8 = (f32[512,768]{1,0:T(8,128)S(1)}, f32[512,768]{1,0:T(8,128)}, u32[]{:S(2)}) copy-start(f32[512,768]{1,0:T(8,128)} %copy-done.7) | copy-start | bytes 4718596
  670.3 49.7 %copy-start.23 = (f32[12,768]{1,0:T(8,128)S(1)}, f32[12,768]{1,0:T(8,128)}, u32[]{:S(2)}) copy-start(f32[12,768]{1,0:T(8,128)} %param.40) | copy-start | bytes 110596
  670.3 49.7 %copy-start.25 = (f32[12,768]{1,0:T(8,128)S(1)}, f32[12,768]{1,0:T(8,128)}, u32[]{:S(2)}) copy-start(f32[12,768]{1,0:T(8,128)} %param.43) | copy-start | bytes 110596
  670.3 51.2 %copy-start.24 = (f32[160,12]{0,1:T(8,128)S(1)}, f32[160,12]{0,1:T(8,128)}, u32[]{:S(2)}) copy-start(f32[160,12]{0,1:T(8,128)} %param.44) | copy-start | bytes 23044
  670.4 51.2 %copy-start.26 = (f32[160,12]{0,1:T(8,128)S(1)}, f32[160,12]{0,1:T(8,128)}, u32[]{:S(2)}) copy-start(f32[160,12]{0,1:T(8,128)} %param.47) | copy-start | bytes 23044
  670.4 51.2 %copy-start.27 = (f32[160,12]{0,1:T(8,128)S(1)}, f32[160,12]{0,1:T(8,128)}, u32[]{:S(2)}) copy-start(f32[160,12]{0,1:T(8,128)} %param.45) | copy-start | bytes 23044
  670.4 52.6 %copy-start.16 = (f32[96,768]{1,0:T(8,128)S(1)}, f32[96,768]{1,0:T(8,128)}, u32[]{:S(2)}) copy-start(f32[96,768]{1,0:T(8,128)} %param.32) | copy-start | bytes 884740
  670.4 52.6 %copy-start.17 = (f32[96,768]{1,0:T(8,128)S(1)}, f32[96,768]{1,0:T(8,128)}, u32[]{:S(2)}) copy-start(f32[96,768]{1,0:T(8,128)} %reduce-scatter.3.cloned.1.call-done) | copy-start | bytes 884740
  670.4 54.9 %copy-start.14 = (f32[192,768]{1,0:T(8,128)S(1)}, f32[192,768]{1,0:T(8,128)}, u32[]{:S(2)}) copy-start(f32[192,768]{1,0:T(8,128)} %param.36) | copy-start | bytes 1769476
  670.4 54.9 %copy-start.15 = (f32[192,768]{1,0:T(8,128)S(1)}, f32[192,768]{1,0:T(8,128)}, u32[]{:S(2)}) copy-start(f32[192,768]{1,0:T(8,128)} %reduce-scatter.5.cloned.1.call-done) | copy-start | bytes 1769476
  (9 other events, 14.3 us)
Sparse Core Ops, SparseCore 0:
  11.5 66.3 all-gather.2
  81.4 79.8 all-gather.4
  316.1 138.9 reduce-scatter.2
  461.4 205.7 reduce-scatter.4
where the time goes:
time: 751 us; the launch traced here: 737 us
  matrix products  270 us (36%)
  waiting for transfers between devices  203 us (27%)
  local copies, waits for them, and re-layouts  106 us (14%)
  other arithmetic  76.5 us (10%)
  blocking collectives  40.4 us (5%)
  loops' own time  21.2 us (3%)
  between operations  20.1 us (3%)
    reduce_scatter x1, waiting for transfers between devices, shards(): lax.psum_scatter(grad_ffn, ('dp', 'fsdp'), scatter_dimension=0, tiled=True)  203 us
    dot_general x16, matrix products, rel_one_block(): jnp.einsum('ijb,bh->ihj', one_hot, table_high, preferred_element_type=jnp...  65.3 us
    dot_general x16, matrix products, table_one_block(): jnp.einsum('ijb,ihj->bh', one_hot, d_block, preferred_element_type=jnp.fl...  64.6 us
    dot_general x16, matrix products, rel_one_block(): jnp.einsum('ijb,bh->ihj', one_hot, table_rest, preferred_element_type=jnp...  47.8 us
    psum x1, blocking collectives, shards(): lax.psum((grad_vectors, grad_table, shard_squares), ('dp', 'fsdp'))  40.4 us
    add x32, other arithmetic, bucket_onehot(): third_hot = (y_rows[..., None] + B1 + BX == bucket_ids).astype(jnp.bfloat16)  28.5 us
    dot_general x1, matrix products, shards(): lax.dot_general(hidden_low, w_first, contract_last, preferred_element_typ...  20.1 us
    dynamic_slice x32, local copies, waits for them, and re-layouts, rel_bias(): blocks = lax.map(rel_one_block, jnp.arange(SEQ // row_block))  18.7 us
  transfers between devices with their start and end apart: 4, of which 1 were waited for; matrix products, arithmetic and copies ran while one was open for 46% of the time, Pallas kernels for 0%

commit v1 on v0

v1 whole, which is shorter than its diff:
```python
import math

import jax
import jax.numpy as jnp
from jax import lax
from jax.experimental import pallas as pl
from jax.experimental.pallas import tpu as pltpu
from jax.sharding import PartitionSpec as P

D = 768
H = 12
HD = 64
FF = 3072
B1 = 32
BX = 64
SEQ = 512
STEP = 10
BUCKETS = B1 + 2 * BX


NEG_FILL = -1e30
NORM_EPS = 1e-05
BF = jnp.bfloat16
F32 = jnp.float32
NT = (((1,), (1,)), ((), ()))
TN = (((0,), (0,)), ((), ()))
NN = (((1,), (0,)), ((), ()))
ALL = ("dp", "fsdp")


def mm(a, b, dims):
    return lax.dot_general(a, b, dims, preferred_element_type=F32)


def adam_update(weight, moment_one, second, gradient, clip_scale, step_rate, decay_rate, average):
    clipped = gradient * clip_scale
    new_first = 0.9 * moment_one + 0.1 * clipped
    new_second = 0.999 * second + 0.001 * clipped * clipped
    first_hat = new_first / (1.0 - 0.9**STEP)
    second_hat = new_second / (1.0 - 0.999**STEP)
    new_weight = weight - step_rate * (
        first_hat / (jnp.sqrt(second_hat) + 1e-08) + decay_rate * weight
    )
    new_average = 0.8 * average + 0.2 * new_weight
    return (new_weight, new_first, new_second, new_average)


def bias_kernel(len_ref, tab_ref, one_ref, x_ref, y_ref, out_ref):
    length = len_ref[0]
    rows = one_ref.shape[1]
    for r in range(0, rows, 8):
        for c in range(0, SEQ, 128):
            ids = [ref[0, r : r + 8, c : c + 128] for ref in (one_ref, x_ref, y_ref)]
            keep = lax.broadcasted_iota(jnp.int32, (8, 128), 1) + c < length
            for h in range(H):
                total = None
                for t in range(3):
                    line = jnp.broadcast_to(tab_ref[h, t : t + 1, :], (8, 128))
                    got = jnp.take_along_axis(line, ids[t], axis=1, mode="promise_in_bounds")
                    total = got if total is None else total + got
                out_ref[h, r : r + 8, c : c + 128] = jnp.where(keep, total, NEG_FILL)


def page_bias(lengths, table, rel_1d, rel_x, rel_y):
    rows = 64
    lines = table.T
    tab = jnp.stack(
        [
            jnp.pad(lines[:, :B1], ((0, 0), (0, 128 - B1))),
            jnp.pad(lines[:, B1 : B1 + BX], ((0, 0), (0, 128 - BX))),
            jnp.pad(lines[:, B1 + BX :], ((0, 0), (0, 128 - BX))),
        ],
        axis=1,
    )
    ids = pl.BlockSpec((1, rows, SEQ), lambda i, *_: (0, i, 0))
    return pl.pallas_call(
        bias_kernel,
        grid_spec=pltpu.PrefetchScalarGridSpec(
            num_scalar_prefetch=1,
            grid=(SEQ // rows,),
            in_specs=[pl.BlockSpec((H, 3, 128), lambda i, *_: (0, 0, 0)), ids, ids, ids],
            out_specs=pl.BlockSpec((H, rows, SEQ), lambda i, *_: (0, i, 0)),
        ),
        out_shape=jax.ShapeDtypeStruct((H, SEQ, SEQ), F32),
        cost_estimate=pl.CostEstimate(
            flops=20_000_000_000, bytes_accessed=16_000_000, transcendentals=0
        ),
        name="bias",
    )(lengths, tab, rel_1d, rel_x, rel_y)


def head_masks():
    lane = lax.broadcasted_iota(jnp.int32, (1, 2 * HD), 1)
    return (lane < HD, lane >= HD)


def attend_kernel(q_ref, k_ref, v_ref, bias_ref, ctx_ref, p_ref, *, rows):
    zero = jnp.zeros((), BF)
    masks = head_masks()
    keys = [jnp.where(m, k_ref[...], zero) for m in masks]
    vals = [jnp.where(m, v_ref[...], zero) for m in masks]
    for r in range(0, SEQ, rows):
        q = q_ref[r : r + rows, :]
        ctx = None
        for h in range(2):
            scores = mm(q, keys[h], NT) * HD ** (-0.5) + bias_ref[h, r : r + rows, :]
            top = jnp.max(scores, axis=-1, keepdims=True)
            raised = jnp.exp(scores - top)
            total = jnp.sum(raised, axis=-1, keepdims=True)
            soft = (raised * (1.0 / total)).astype(BF)
            p_ref[h, r : r + rows, :] = soft
            part = mm(soft, vals[h], NN)
            ctx = part if ctx is None else ctx + part
        ctx_ref[r : r + rows, :] = ctx.astype(BF)


def lane_block(offset):
    return pl.BlockSpec((SEQ, 2 * HD), lambda i: (0, offset + i))


PAIR_BLOCK = pl.BlockSpec((2, SEQ, SEQ), lambda i: (i, 0, 0))


def attend(qkv, bias):
    n = D // (2 * HD)
    return pl.pallas_call(
        lambda *refs: attend_kernel(*refs, rows=256),
        grid=(n,),
        in_specs=[lane_block(0), lane_block(n), lane_block(2 * n), PAIR_BLOCK],
        out_specs=[lane_block(0), PAIR_BLOCK],
        out_shape=[
            jax.ShapeDtypeStruct((SEQ, D), BF),
            jax.ShapeDtypeStruct((H, SEQ, SEQ), BF),
        ],
        cost_estimate=pl.CostEstimate(
            flops=10_000_000_000, bytes_accessed=22_000_000, transcendentals=3_200_000
        ),
        name="attend",
    )(qkv, qkv, qkv, bias)


def attend_back_kernel(
    q_ref, k_ref, v_ref, p_ref, c_ref, dc_ref, dq_ref, dk_ref, dv_ref, ds_ref, sum_ref, *, rows
):
    zero = jnp.zeros((), BF)
    masks = head_masks()
    keys = [jnp.where(m, k_ref[...], zero) for m in masks]
    vals = [jnp.where(m, v_ref[...], zero) for m in masks]
    scale = HD ** (-0.5)
    q_sum = jnp.zeros((1, 2 * HD), F32)
    for r in range(0, SEQ, rows):
        dc = dc_ref[r : r + rows, :]
        prod = dc.astype(F32) * c_ref[r : r + rows, :].astype(F32)
        dq = None
        for h in range(2):
            soft = p_ref[h, r : r + rows, :]
            inner = jnp.sum(jnp.where(masks[h], prod, 0.0), axis=-1, keepdims=True)
            d_soft = mm(dc, vals[h], NT)
            d_scores = (soft.astype(F32) * (d_soft - inner)).astype(BF)
            ds_ref[h, r : r + rows, :] = d_scores
            part = mm(d_scores, keys[h], NN)
            dq = part if dq is None else dq + part
        dq = (dq * scale).astype(BF)
        dq_ref[r : r + rows, :] = dq
        q_sum = q_sum + jnp.sum(dq.astype(F32), axis=0, keepdims=True)
    flips = (dc_ref[...].astype(F32).T.astype(BF), q_ref[...].astype(F32).T.astype(BF))
    sums = [q_sum]
    for flip, factor, pair_ref, out_ref in (
        (flips[0], 1.0, p_ref, dv_ref),
        (flips[1], scale, ds_ref, dk_ref),
    ):
        parts = [mm(flip[HD * h : HD * h + HD, :], pair_ref[h], NN) for h in range(2)]
        done = (jnp.concatenate(parts, axis=0).T * factor).astype(BF)
        out_ref[...] = done
        sums.append(jnp.sum(done.astype(F32), axis=0, keepdims=True))
    sum_ref[...] = jnp.concatenate(sums[:2] + [jnp.zeros((6, 2 * HD), F32)], axis=0)


def attend_back(qkv, soft, ctx, d_ctx):
    n = D // (2 * HD)
    return pl.pallas_call(
        lambda *refs: attend_back_kernel(*refs, rows=256),
        grid=(n,),
        in_specs=[
            lane_block(0),
            lane_block(n),
            lane_block(2 * n),
            PAIR_BLOCK,
            lane_block(0),
            lane_block(0),
        ],
        out_specs=[
            lane_block(0),
            lane_block(0),
            lane_block(0),
            PAIR_BLOCK,
            pl.BlockSpec((8, 2 * HD), lambda i: (0, i)),
        ],
        out_shape=[jax.ShapeDtypeStruct((SEQ, D), BF)] * 3
        + [jax.ShapeDtypeStruct((H, SEQ, SEQ), BF), jax.ShapeDtypeStruct((8, D), F32)],
        cost_estimate=pl.CostEstimate(
            flops=9_000_000_000, bytes_accessed=16_000_000, transcendentals=0
        ),
        name="attend_back",
    )(qkv, qkv, qkv, soft, ctx, d_ctx)


def table_kernel(one_ref, x_ref, y_ref, ds_ref, out_ref):
    @pl.when(pl.program_id(0) == 0)
    def _():
        out_ref[...] = jnp.zeros_like(out_ref)

    rows = one_ref.shape[1]
    flipped = jnp.swapaxes(ds_ref[...].astype(F32), 0, 1).astype(BF)
    total = None
    for r in range(rows):
        hot = jnp.concatenate(
            [
                (lax.broadcasted_iota(jnp.int32, (size, SEQ), 0) == ref[0, r : r + 1, :])
                .astype(F32)
                .astype(BF)
                for ref, size in ((one_ref, B1), (x_ref, BX), (y_ref, BX))
            ],
            axis=0,
        )
        part = mm(flipped[r], hot, NT)
        total = part if total is None else total + part
    out_ref[...] += total


def table_grad(rel_1d, rel_x, rel_y, d_scores):
    rows = 16
    ids = pl.BlockSpec((1, rows, SEQ), lambda i: (0, i, 0))
    return pl.pallas_call(
        table_kernel,
        grid=(SEQ // rows,),
        in_specs=[ids, ids, ids, pl.BlockSpec((H, rows, SEQ), lambda i: (0, i, 0))],
        out_specs=pl.BlockSpec((H, BUCKETS), lambda i: (0, 0)),
        out_shape=jax.ShapeDtypeStruct((H, BUCKETS), F32),
        cost_estimate=pl.CostEstimate(
            flops=22_000_000_000, bytes_accessed=10_000_000, transcendentals=0
        ),
        name="table_grad",
    )(rel_1d, rel_x, rel_y, d_scores)


def row_mean(values):
    return jnp.mean(values, axis=-1, keepdims=True)


def normal_rows(values):
    center = values - row_mean(values)
    inv = lax.rsqrt(row_mean(center * center) + NORM_EPS)
    return center * inv, inv


def normal_back(normal, inv, grad):
    return inv * (grad - row_mean(grad) - normal * row_mean(grad * normal))


def gelu_parts(u):
    z = jnp.abs(u) * (2.0**-0.5)
    t = 1.0 / (1.0 + 0.3275911 * z)
    tail = jnp.exp(-0.5 * u * u)
    poly = t * (
        0.254829592
        + t * (-0.284496736 + t * (1.421413741 + t * (-1.453152027 + t * 1.061405429)))
    )
    half = 0.5 * poly * tail
    cdf = jnp.where(u < 0, half, 1.0 - half)
    return u * cdf, cdf + u * (tail * (1.0 / math.sqrt(2.0 * math.pi)))


def row_sum(values):
    return jnp.sum(values.astype(F32), axis=0, keepdims=True)


def block_kernel(
    ctx_ref,
    tok_ref,
    cot_ref,
    vec_ref,
    b1_ref,
    wo_ref,
    w1_ref,
    w2_ref,
    out_ref,
    hid_ref,
    act_ref,
    dff_ref,
    du_ref,
    dr_ref,
    dab_ref,
    dctx_ref,
    sum_ref,
    db1_ref,
    slope_ref,
    *,
    wide,
):
    @pl.when(pl.program_id(0) == 0)
    def _():
        sum_ref[...] = jnp.zeros_like(sum_ref)
        db1_ref[...] = jnp.zeros_like(db1_ref)

    vec = [vec_ref[i : i + 1, :] for i in range(8)]
    resid = tok_ref[...].astype(F32) + (mm(ctx_ref[...], wo_ref[...], NN) + vec[6])
    n_one, inv_one = normal_rows(resid)
    hidden = n_one * vec[0] + vec[1]
    hid_low = hidden.astype(BF)
    hid_ref[...] = hid_low
    total = hidden + vec[7]
    for f in range(0, FF, wide):
        part = slice(f, f + wide)
        u = mm(hid_low, w1_ref[part, :], NT) + b1_ref[:, part]
        act, slope = gelu_parts(u)
        act = act.astype(BF)
        act_ref[:, part] = act
        slope_ref[:, part] = slope
        total = total + mm(act, w2_ref[part, :], NN)
    n_two, inv_two = normal_rows(total)
    out_ref[...] = (n_two * vec[2] + vec[3]).astype(BF)
    dy = cot_ref[...].astype(F32)
    d_two = normal_back(n_two, inv_two, dy * vec[2])
    dff = d_two.astype(BF)
    dff_ref[...] = dff
    d_hid = d_two
    for f in range(0, FF, wide):
        part = slice(f, f + wide)
        du = (mm(dff, w2_ref[part, :], NT) * slope_ref[:, part]).astype(BF)
        du_ref[:, part] = du
        db1_ref[:, part] += row_sum(du)
        d_hid = d_hid + mm(du, w1_ref[part, :], NN)
    d_one = normal_back(n_one, inv_one, d_hid * vec[0])
    dr_ref[...] = d_one
    dab = d_one.astype(BF)
    dab_ref[...] = dab
    dctx_ref[...] = mm(dab, wo_ref[...], NT).astype(BF)
    sum_ref[...] += jnp.concatenate(
        [
            row_sum(d_hid * n_one),
            row_sum(d_hid),
            row_sum(dy * n_two),
            row_sum(dy),
            jnp.zeros((2, D), F32),
            row_sum(dab),
            row_sum(dff),
        ],
        axis=0,
    )


def block_pass(ctx, tokens, cotangent, vectors, b_first, w_out, w_first, w_second):
    rows = 128
    by_row = lambda width: pl.BlockSpec((rows, width), lambda i: (i, 0))
    whole = lambda shape: pl.BlockSpec(shape, lambda i: (0, 0), pipeline_mode=pl.Buffered(1))
    count = tokens.shape[0]
    low = lambda width: jax.ShapeDtypeStruct((count, width), BF)
    return pl.pallas_call(
        lambda *refs: block_kernel(*refs, wide=768),
        grid=(count // rows,),
        in_specs=[
            by_row(D),
            by_row(D),
            by_row(D),
            whole((12, D)),
            whole((1, FF)),
            whole((D, D)),
            whole((FF, D)),
            whole((FF, D)),
        ],
        out_specs=[
            by_row(D),
            by_row(D),
            by_row(FF),
            by_row(D),
            by_row(FF),
            by_row(D),
            by_row(D),
            by_row(D),
            pl.BlockSpec((8, D), lambda i: (0, 0)),
            pl.BlockSpec((1, FF), lambda i: (0, 0)),
        ],
        out_shape=[
            low(D),
            low(D),
            low(FF),
            low(D),
            low(FF),
            jax.ShapeDtypeStruct((count, D), F32),
            low(D),
            low(D),
            jax.ShapeDtypeStruct((8, D), F32),
            jax.ShapeDtypeStruct((1, FF), F32),
        ],
        scratch_shapes=[pltpu.VMEM((rows, FF), F32)],
        cost_estimate=pl.CostEstimate(
            flops=20_000_000_000, bytes_accessed=22_000_000, transcendentals=1_600_000
        ),
        name="block_pass",
    )(ctx, tokens, cotangent, vectors, b_first, w_out, w_first, w_second)


def shards(
    tokens,
    cotangent,
    lengths,
    rel_1d,
    rel_x,
    rel_y,
    attn_weights,
    attn_m1,
    attn_m2,
    attn_ema,
    ffn_weights,
    ffn_m1,
    ffn_m2,
    ffn_ema,
    vectors,
    vec_m1,
    vec_m2,
    vec_ema,
    table,
    tab_m1,
    tab_m2,
    tab_ema,
):
    attn_full, ffn_full = (
        lax.all_gather(attn_weights.astype(BF), ALL, axis=0, tiled=True),
        lax.all_gather(ffn_weights.astype(BF), ALL, axis=0, tiled=True),
    )
    w_three, w_out = attn_full[: 3 * D].reshape(3, D, D), attn_full[3 * D :]
    w_first, w_second = ffn_full[:FF], ffn_full[FF:]
    bias = page_bias(lengths, table, rel_1d, rel_x, rel_y)
    add_three = jnp.concatenate([vectors[4], jnp.zeros((D,), F32), vectors[5]])
    qkv = jnp.concatenate([mm(tokens, w_three[t], NN) for t in range(3)], axis=1)
    qkv = (qkv + add_three).astype(BF)
    ctx, soft = attend(qkv, bias)
    (
        block_out,
        hid_low,
        act_low,
        d_ffn,
        d_pre_low,
        d_resid_one,
        d_attn,
        d_context,
        sums,
        grad_bias_first,
    ) = block_pass(
        ctx, tokens, cotangent, vectors, vectors[8:].reshape(1, FF), w_out, w_first, w_second
    )
    grad_ffn = jnp.concatenate(
        [mm(d_pre_low, hid_low, TN).astype(BF), mm(act_low, d_ffn, TN).astype(BF)], axis=0
    )
    dq, dk, dv, d_scores, qv_sums = attend_back(qkv, soft, ctx, d_context)
    d_three = (dq, dk, dv)
    grad_attn = jnp.concatenate(
        [mm(tokens, d, TN).astype(BF) for d in d_three] + [mm(ctx, d_attn, TN).astype(BF)], axis=0
    )
    grad_input = d_resid_one
    for t in range(3):
        grad_input = grad_input + mm(d_three[t], w_three[t], NT)
    grad_table = table_grad(rel_1d, rel_x, rel_y, d_scores).T
    attn_shard, ffn_shard = (
        lax.psum_scatter(grad_attn, ALL, scatter_dimension=0, tiled=True).astype(F32),
        lax.psum_scatter(grad_ffn, ALL, scatter_dimension=0, tiled=True).astype(F32),
    )
    grad_vectors = jnp.concatenate(
        [sums[:4], qv_sums[:2], sums[6:], grad_bias_first.reshape(FF // D, D)], axis=0
    )
    shard_squares = jnp.sum(attn_shard * attn_shard) + jnp.sum(ffn_shard * ffn_shard)
    vec_total, tab_total, square_total = lax.psum(
        (grad_vectors, grad_table, shard_squares), ALL
    )
    grad_norm = jnp.sqrt(
        square_total + jnp.sum(vec_total * vec_total) + jnp.sum(tab_total * tab_total)
    )
    clip_scale = 1.0 / jnp.maximum(grad_norm, 1.0)
    attn_new = adam_update(
        attn_weights, attn_m1, attn_m2, attn_shard, clip_scale, 0.06, 0.01, attn_ema
    )
    ffn_new = adam_update(ffn_weights, ffn_m1, ffn_m2, ffn_shard, clip_scale, 0.06, 0.01, ffn_ema)
    vec_new = adam_update(vectors, vec_m1, vec_m2, vec_total, clip_scale, 0.6, 0.0, vec_ema)
    tab_new = adam_update(table, tab_m1, tab_m2, tab_total, clip_scale, 0.6, 0.0, tab_ema)
    return (
        block_out,
        grad_input,
        grad_norm,
        attn_new[0],
        attn_new[1],
        attn_new[2],
        attn_new[3],
        ffn_new[0],
        ffn_new[1],
        ffn_new[2],
        ffn_new[3],
        vec_new[0],
        vec_new[1],
        vec_new[2],
        vec_new[3],
        tab_new[0],
        tab_new[1],
        tab_new[2],
        tab_new[3],
        vec_total * clip_scale,
    )


def solution(mesh):
    return jax.shard_map(
        shards,
        mesh=mesh,
        in_specs=(
            P(("dp", "fsdp"), None),
            P(("dp", "fsdp"), None),
            P(("dp", "fsdp")),
            P(("dp", "fsdp"), None, None),
            P(("dp", "fsdp"), None, None),
            P(("dp", "fsdp"), None, None),
            P(("dp", "fsdp"), None),
            P(("dp", "fsdp"), None),
            P(("dp", "fsdp"), None),
            P(("dp", "fsdp"), None),
            P(("dp", "fsdp"), None),
            P(("dp", "fsdp"), None),
            P(("dp", "fsdp"), None),
            P(("dp", "fsdp"), None),
            P(),
            P(),
            P(),
            P(),
            P(),
            P(),
            P(),
            P(),
        ),
        out_specs=(
            P(("dp", "fsdp"), None),
            P(("dp", "fsdp"), None),
            P(),
            P(("dp", "fsdp"), None),
            P(("dp", "fsdp"), None),
            P(("dp", "fsdp"), None),
            P(("dp", "fsdp"), None),
            P(("dp", "fsdp"), None),
            P(("dp", "fsdp"), None),
            P(("dp", "fsdp"), None),
            P(("dp", "fsdp"), None),
            P(),
            P(),
            P(),
            P(),
            P(),
            P(),
            P(),
            P(),
            P(),
        ),
        check_vma=False,
    )
```

time: 751 us -> 534 us (0.71); the launches traced: 737 us -> 532 us
  matrix products: 270 us -> 23.6 us
  Pallas kernels: 0 us -> 115 us
  local copies, waits for them, and re-layouts: 106 us -> 16.8 us
  waiting for transfers between devices: 203 us -> 278 us
  other arithmetic: 76.5 us -> 37.5 us
  loops' own time: 21.2 us -> 0 us
    dot_general x66 -> x12, matrix products: 270 us -> 23.6 us  [mm(): return lax.dot_general(a, b, dims, preferred_element_type=F32)]
    pallas_call x0 -> x5, Pallas kernels: none -> 115 us  [the longest x1 34.7 us: block_pass(): pl.pallas_call(lambda *refs: block_kernel(*refs, wide=768), grid=(count /...]
    all_gather x2, waiting for transfers between devices: 0.02 us -> 97.9 us  [the longest x1 62.3 us: shards(): lax.all_gather(ffn_weights.astype(BF), ALL, axis=0, tiled=True)]
    dynamic_slice x64 -> x0, local copies, waits for them, and re-layouts: 46 us -> none  [the longest x32 18.7 us: rel_bias(): blocks = lax.map(rel_one_block, jnp.arange(SEQ // row_block))]
    add x33 -> x0, other arithmetic: 28.5 us -> none  [the longest x32 28.5 us: bucket_onehot(): third_hot = (y_rows[..., None] + B1 + BX == bucket_ids).astype(jnp.bfloat16)]
    reduce_scatter x2, waiting for transfers between devices: 203 us -> 180 us  [the longest x1 139 us: shards(): lax.psum_scatter(grad_ffn, ALL, scatter_dimension=0, tiled=True).astype(F32)]
    another operation x2 -> x0, loops' own time: 21.2 us -> none  [the longest x1 10.6 us: table_grad(): lax.map(table_one_block, jnp.arange(SEQ // row_block))]
    reshape x5 -> x0, local copies, waits for them, and re-layouts: 16.9 us -> none  [the longest x1 16.9 us: rel_bias(): return blocks.reshape(SEQ, H, SEQ)]
  transfers between devices with their start and end apart: 4 -> 4, of which waited for: 1 -> 4; matrix products, arithmetic and copies ran while one was open for 46% -> 9% of each run, Pallas kernels for 0% -> 13%
where the time goes in v1:
time: 534 us; the launch traced here: 532 us
  waiting for transfers between devices  278 us (52%)
  Pallas kernels  115 us (22%)
  blocking collectives  41.1 us (8%)
  other arithmetic  37.5 us (7%)
  matrix products  23.6 us (4%)
  between operations  19.2 us (4%)
  local copies, waits for them, and re-layouts  16.8 us (3%)
    reduce_scatter x1, waiting for transfers between devices, shards(): lax.psum_scatter(grad_ffn, ALL, scatter_dimension=0, tiled=True).astype(F32)  139 us
    all_gather x1, waiting for transfers between devices, shards(): lax.all_gather(ffn_weights.astype(BF), ALL, axis=0, tiled=True)  62.3 us
    psum x1, blocking collectives, shards(): lax.psum((grad_vectors, grad_table, shard_squares), ALL)  41.1 us
    reduce_scatter x1, waiting for transfers between devices, shards(): lax.psum_scatter(grad_attn, ALL, scatter_dimension=0, tiled=True)  40.7 us
    all_gather x1, waiting for transfers between devices, shards(): lax.all_gather(attn_weights.astype(BF), ALL, axis=0, tiled=True)  35.5 us
    pallas_call x1, Pallas kernels, block_pass(): pl.pallas_call(lambda *refs: block_kernel(*refs, wide=768), grid=(count /...  34.7 us
    pallas_call x1, Pallas kernels, table_grad(): pl.pallas_call(table_kernel, grid=(SEQ // rows,), in_specs=[ids, ids, ids...  30.5 us
    pallas_call x1, Pallas kernels, page_bias(): pl.pallas_call(bias_kernel, grid_spec=pltpu.PrefetchScalarGridSpec(num_sc...  26.3 us
  transfers between devices with their start and end apart: 4, of which 4 were waited for; matrix products, arithmetic and copies ran while one was open for 9% of the time, Pallas kernels for 13%

profile of v1, /device:TPU:0, one launch (start us, length us, event | category | flops | bytes accessed | tf_op | source)
XLA Modules:
  0.0 531.8 jit_solution(11857429032787503886)
XLA Ops:
  7.2 1.6 convert_element_type.47
  9.0 1.8 convert_element_type.49
  16.0 26.3 %bias.1.refs_3_ = f32[12,512,512]{2,1,0:T(8,128)} custom-call(s32[1]{0:T(128)S(6)} %copy.45.len_ref, f32[12,3,128]{2,1,0:T(4,128)} %pad_maximum_fusion.3.tab_ref, s32[1,512,512]{2,1,0:T(8,128)} %one_ref.3, s32[1,512,512]{2,1,0:T(8,128)} %x_ref.3, s32[1,512,512]{2,1,0:T(8,128)} %y_ref.3), custom_call_target="tpu_custom_call" | custom-call | flops 20000000000 | bytes 16000000 | tf_op jit(solution)/shard_map/bias/pallas_call | solution.py:76
  42.3 35.5 %all-gather.3.cloned.1.call-done = bf16[3072,768]{1,0:T(8,128)(2,1)} async-done(((bf16[96,768]{1,0:T(8,128)(2,1)}), bf16[3072,768]{1,0:T(8,128)(2,1)}) %all-gather.3.cloned.1.call-update) | async-done | bytes 4718608 | tf_op jit(solution)/shard_map/all_gather | solution.py:429
  77.8 2.5 slice.77.refs_5_
  80.3 2.0 fusion.13
  84.0 1.8 fusion.refs_0_.refs_1_.refs_2_
  85.7 12.9 %attend.1 = (bf16[512,768]{1,0:T(8,128)(2,1)}, bf16[12,512,512]{2,1,0:T(8,128)(2,1)}) custom-call(bf16[512,2304]{1,0:T(8,128)(2,1)} %fusion.refs_0_.refs_1_.refs_2_, bf16[512,2304]{1,0:T(8,128)(2,1)} %fusion.refs_0_.refs_1_.refs_2_, bf16[512,2304]{1,0:T(8,128)(2,1)} %fusion.refs_0_.refs_1_.refs_2_, f32[12,512,512]{2,1,0:T(8,128)} %bias.1.refs_3_), custom_call_target="tpu_custom_call" | custom-call | flops 10000000000 | bytes 22000000 | tf_op jit(solution)/shard_map/attend/pallas_call | solution.py:126
  98.6 62.3 %all-gather.5.cloned.1.call-done = bf16[6144,768]{1,0:T(8,128)(2,1)} async-done(((bf16[192,768]{1,0:T(8,128)(2,1)}), bf16[6144,768]{1,0:T(8,128)(2,1)}) %all-gather.5.cloned.1.call-update) | async-done | bytes 9437200 | tf_op jit(solution)/shard_map/all_gather | solution.py:430
  160.9 8.0 %fusion.32 = (bf16[3072,768]{1,0:T(8,128)(2,1)}, bf16[3072,768]{1,0:T(8,128)(2,1)}) fusion(bf16[6144,768]{1,0:T(8,128)(2,1)} %all-gather.5.cloned.1.call-done), kind=kLoop, calls=%fused_computation.65 | loop fusion | bytes 18874368 | tf_op jit(solution)/shard_map/slice | solution.py:433
  169.0 34.7 %block_pass.1 = (bf16[512,768]{1,0:T(8,128)(2,1)}, bf16[512,768]{1,0:T(8,128)(2,1)}, bf16[512,3072]{1,0:T(8,128)(2,1)}, bf16[512,768]{1,0:T(8,128)(2,1)}, bf16[5...) custom-call(bf16[512,768]{1,0:T(8,128)(2,1)} %get-tuple-element.37.r, ...), custom_call_target="tpu_custom_call" | custom-call | flops 20000000000 | bytes 22000000 | tf_op jit(solution)/shard_map/block_pass/pallas_call | solution.py:359
  203.7 11.0 %attend_back.1 = (bf16[512,768]{1,0:T(8,128)(2,1)}, bf16[512,768]{1,0:T(8,128)(2,1)}, bf16[512,768]{1,0:T(8,128)(2,1)}, bf16[12,512,512]{2,1,0:T(8,128)(2,1)}, f32[8,768]{1,0:T(8,128)}) custom-call(bf16[512,2304]{1,0:T(8,128)(2,1)} %fusion.refs_0_.refs_1_.refs_2_, bf16[512,2304]{1,0:T(8,128)(2,1)} %fusion.refs_0_.refs_1_.refs_2_, ...), custom_call_target="tpu_custom_call" | custom-call | flops 8999999488 | bytes 16000000 | tf_op jit(solution)/shard_map/attend_back/pallas_call | solution.py:181
  214.7 2.1 fusion.1
  219.3 2.5 pad_maximum_fusion.1
  221.9 1.1 copy-done.24
  223.0 4.7 convolution_convert_fusion.1
  227.7 3.1 convolution_convert_fusion
  230.8 15.6 %pad_maximum_fusion = bf16[6144,768]{1,0:T(8,128)(2,1)} fusion(bf16[3072,768]{1,0:T(8,128)(2,1)S(1)} %convolution_convert_fusion, bf16[3072,768]{1,0:T(8,128)(2,1)S(1)} %convolution_convert_fusion.1), kind=kLoop, calls=%fused_computation | loop fusion | flops 18874368 | bytes 18874368 | tf_op jit(solution)/shard_map/concatenate | solution.py:453
  249.2 2.2 fusion.11
  251.4 2.1 fusion.7
  253.5 3.3 add_add_fusion
  256.9 30.5 %table_grad.1 = f32[12,160]{1,0:T(8,128)} custom-call(s32[1,512,512]{2,1,0:T(8,128)} %one_ref.3, s32[1,512,512]{2,1,0:T(8,128)} %x_ref.3, s32[1,512,512]{2,1,0:T(8,128)} %y_ref.3, bf16[12,512,512]{2,1,0:T(8,128)(2,1)} %get-tuple-element.53.ds_ref), custom_call_target="tpu_custom_call" | custom-call | flops 22000001024 | bytes 10000000 | tf_op jit(solution)/shard_map/table_grad/pallas_call | solution.py:234
  287.4 40.7 %reduce-scatter.3.cloned.1.call-done = bf16[96,768]{1,0:T(8,128)(2,1)} async-done(((bf16[3072,768]{1,0:T(8,128)(2,1)}), bf16[96,768]{1,0:T(8,128)(2,1)}) %reduce-scatter.3.cloned.1.call-update) | async-done | bytes 147472 | tf_op jit(solution)/shard_map/reduce_scatter | solution.py:466
  328.1 1.7 fusion.21
  329.8 139.3 %reduce-scatter.5.cloned.1.call-done = bf16[192,768]{1,0:T(8,128)(2,1)} async-done(((bf16[6144,768]{1,0:T(8,128)(2,1)}), bf16[192,768]{1,0:T(8,128)(2,1)}) %reduce-scatter.5.cloned.1.call-update) | async-done | bytes 294928 | tf_op jit(solution)/shard_map/reduce_scatter | solution.py:467
  469.0 1.7 fusion.17
  472.1 41.1 %all-reduce.2 = (f32[]{:T(128)}, f32[12,768]{1,0:T(8,128)S(1)}, f32[160,12]{0,1:T(8,128)}) all-reduce(f32[]{:T(128)S(6)} %add.117, f32[12,768]{1,0:T(8,128)S(1)} %pad_maximum_fusion.2, f32[160,12]{0,1:T(8,128)} %bitcast.36), channel_id=1, replica_groups=mesh['dp'=8,'fsdp'=4] {'dp','fsdp'}, use_global_device_ids=true, to_apply=%region_4.5 | all-reduce | flops 11137 | bytes 89096 | tf_op jit(solution)/shard_map/psum | solution.py:473
  513.8 1.3 multiply_reduce_fusion.1
  517.2 1.5 multiply_add_fusion.4
  518.6 1.5 multiply_add_fusion.2
  520.2 2.7 multiply_add_fusion
  522.9 1.2 multiply_add_fusion.1
  (83 shorter events, 12.1 us)
Async XLA Ops:
  7.2 70.6 %all-gather.3.cloned.1.call-start = ((), (), s32[]{:S(2)}) async-start(), calls=%async_computation.2 | async-start | bytes 4866048 | tf_op jit(solution)/shard_map/all_gather | solution.py:429
  8.9 152.0 %all-gather.5.cloned.1.call-start = ((), (), s32[]{:S(2)}) async-start(), calls=%async_computation.3 | async-start | bytes 9732096 | tf_op jit(solution)/shard_map/all_gather | solution.py:430
  10.8 317.3 %reduce-scatter.3.cloned.1.call-start = ((), (), s32[]{:S(2)}) async-start(), calls=%async_computation.4 | async-start | bytes 4866048 | tf_op jit(solution)/shard_map/reduce_scatter | solution.py:466
  16.0 64.3 %copy-start.16 = (bf16[512,768]{1,0:T(8,128)(2,1)S(1)}, bf16[512,768]{1,0:T(8,128)(2,1)}, u32[]{:S(2)}) copy-start(bf16[512,768]{1,0:T(8,128)(2,1)} %refs_1_.1) | copy-start | bytes 2359300
  77.8 4.6 copy-start.2
  203.7 11.0 %copy-start.17 = (bf16[512,768]{1,0:T(8,128)(2,1)S(1)}, bf16[512,768]{1,0:T(8,128)(2,1)}, u32[]{:S(2)}) copy-start(bf16[512,768]{1,0:T(8,128)(2,1)} %refs_1_.1) | copy-start | bytes 2359300
  214.7 2.1 copy-start.18
  214.7 2.9 copy-start.4
  216.8 1.7 copy-start.20
  216.8 1.7 copy-start.21
  221.8 1.1 copy-start.24
  221.8 247.2 %reduce-scatter.5.cloned.1.call-start = ((), (), s32[]{:S(2)}) async-start(), calls=%async_computation.5 | async-start | bytes 9732096 | tf_op jit(solution)/shard_map/reduce_scatter | solution.py:467
  222.9 4.7 copy-start.22
  223.0 4.7 copy-start.23
  246.4 0.7 copy-start.14
  246.4 2.0 copy-start.15
  246.4 2.7 copy-start.19
  249.2 4.4 copy-start.1
  256.8 260.3 %copy-start.12 = (f32[160,12]{0,1:T(8,128)S(1)}, f32[160,12]{0,1:T(8,128)}, u32[]{:S(2)}) copy-start(f32[160,12]{0,1:T(8,128)} %param.40) | copy-start | bytes 23044
  256.8 261.8 %copy-start.13 = (f32[12,768]{1,0:T(8,128)S(1)}, f32[12,768]{1,0:T(8,128)}, u32[]{:S(2)}) copy-start(f32[12,768]{1,0:T(8,128)} %refs_3_.1) | copy-start | bytes 110596
  256.8 263.3 %copy-start = (f32[192,768]{1,0:T(8,128)S(1)}, f32[192,768]{1,0:T(8,128)}, u32[]{:S(2)}) copy-start(f32[192,768]{1,0:T(8,128)} %param.32) | copy-start | bytes 1769476
  256.8 263.3 %copy-start.5 = (f32[192,768]{1,0:T(8,128)S(1)}, f32[192,768]{1,0:T(8,128)}, u32[]{:S(2)}) copy-start(f32[192,768]{1,0:T(8,128)} %param.35) | copy-start | bytes 1769476
  256.8 263.3 %copy-start.6 = (f32[192,768]{1,0:T(8,128)S(1)}, f32[192,768]{1,0:T(8,128)}, u32[]{:S(2)}) copy-start(f32[192,768]{1,0:T(8,128)} %param.33) | copy-start | bytes 1769476
  256.9 263.3 %copy-start.7 = (f32[192,768]{1,0:T(8,128)S(1)}, f32[192,768]{1,0:T(8,128)}, u32[]{:S(2)}) copy-start(f32[192,768]{1,0:T(8,128)} %param.34) | copy-start | bytes 1769476
  287.4 235.5 %copy-start.3 = (f32[96,768]{1,0:T(8,128)S(1)}, f32[96,768]{1,0:T(8,128)}, u32[]{:S(2)}) copy-start(f32[96,768]{1,0:T(8,128)} %param.28) | copy-start | bytes 884740
  287.4 235.5 %copy-start.9 = (f32[96,768]{1,0:T(8,128)S(1)}, f32[96,768]{1,0:T(8,128)}, u32[]{:S(2)}) copy-start(f32[96,768]{1,0:T(8,128)} %param.31) | copy-start | bytes 884740
  287.4 235.5 %copy-start.10 = (f32[96,768]{1,0:T(8,128)S(1)}, f32[96,768]{1,0:T(8,128)}, u32[]{:S(2)}) copy-start(f32[96,768]{1,0:T(8,128)} %param.29) | copy-start | bytes 884740
  328.1 194.8 %copy-start.8 = (bf16[96,768]{1,0:T(8,128)(2,1)S(1)}, bf16[96,768]{1,0:T(8,128)(2,1)}, u32[]{:S(2)}) copy-start(bf16[96,768]{1,0:T(8,128)(2,1)} %reduce-scatter.3.cloned.1.call-done) | copy-start | bytes 442372
  517.2 5.8 %copy-start.11 = (f32[96,768]{1,0:T(8,128)S(1)}, f32[96,768]{1,0:T(8,128)}, u32[]{:S(2)}) copy-start(f32[96,768]{1,0:T(8,128)} %param.30) | copy-start | bytes 884740
Sparse Core Ops, SparseCore 0:
  11.5 66.2 all-gather.2
  81.3 79.6 all-gather.4
  222.0 106.1 reduce-scatter.2
  333.9 135.1 reduce-scatter.4
